TPU v7x, 32 devices: a whole 2x2x4 slice. The times are simulated.
32 devices in a mesh: lat: 8 (over z, core), lon: 4 (over y, x).
Axes of the slice: x: 2, y: 2, z: 4, core: 2. Of those that a mesh axis runs over, the one named last changes fastest.
Arguments:
- predicted_state: float32 [1440, 13312], P('lon', 'lat'), may hold values from -24 to 24
- verified_state: float32 [1440, 13312], P('lon', 'lat'), may hold values from -20 to 20
- normal_state: float32 [1440, 13312], P('lon', 'lat'), may hold values from -3 to 3
Outputs:
- energy_curves: float32 [3, 52, 721], replicated
- rms_error: float32 [52], replicated
- anomaly_corr: float32 [52], replicated
All inputs are finite; a program needn't handle non-finite values.
Results may differ from a plain program's by a relative error of at most 0.00005.
Values sent between devices are 32-bit elements; how exact they have to be, the bound alone decides.
A program may use at most 64 MiB of HBM per device.

v0:
```python
import jax
import jax.numpy as jnp
from jax import lax
from jax.sharding import PartitionSpec as P

FIELDS = 52
epsilon = 1e-06


def latitude_weights(lat_index, parallel_number):
    return jnp.cos(jnp.pi * ((lat_index.astype(jnp.float32) + 0.5) / parallel_number - 0.5))


def dft_table(lon_rows, lon_total, wave_count):
    longitudes = jnp.arange(lon_rows, dtype=jnp.int32)
    waves = jnp.arange(wave_count, dtype=jnp.int32)
    phase = longitudes[:, None] * waves[None, :] % lon_total
    angle = 2.0 * jnp.pi / lon_total * phase.astype(jnp.float32)
    return jnp.concatenate([jnp.cos(angle), -jnp.sin(angle)], axis=1)


def transform_columns(stacked, table):
    return lax.dot_general(
        stacked,
        table,
        (((0,), (0,)), ((), ())),
        precision=lax.Precision.HIGHEST,
        preferred_element_type=jnp.float32,
    )


def row_powers(fore_coeffs, true_coeffs, wave_count):
    diff_coeffs = fore_coeffs - true_coeffs

    def square(coeffs):
        return (
            coeffs[:, :wave_count] * coeffs[:, :wave_count]
            + coeffs[:, wave_count:] * coeffs[:, wave_count:]
        )

    return jnp.stack([square(fore_coeffs), square(true_coeffs), square(diff_coeffs)], axis=1)


def local(predicted_state, verified_state, normal_state):
    quantity_labels = FIELDS
    meridian_lines, meridian_number = predicted_state.shape
    parallel_lines = meridian_number // quantity_labels
    parallel_number = parallel_lines * lax.axis_size("lat")
    lon_devices = lax.axis_size("lon")
    lon_total = meridian_lines * lon_devices
    wave_count = lon_total // 2 + 1
    row_share = meridian_number // lon_devices
    lat_first = lax.axis_index("lat") * parallel_lines
    weights = latitude_weights(
        lat_first + jnp.arange(parallel_lines, dtype=jnp.int32), parallel_number
    )
    weight_total = jnp.sum(
        latitude_weights(jnp.arange(parallel_number, dtype=jnp.int32), parallel_number)
    )
    predicted_block = predicted_state.reshape(meridian_lines, parallel_lines, quantity_labels)
    observed_block = verified_state.reshape(meridian_lines, parallel_lines, quantity_labels)
    normal_block = normal_state.reshape(meridian_lines, parallel_lines, quantity_labels)
    mismatch_parts = predicted_block - observed_block
    predicted_anomalies = predicted_block - normal_block
    observed_anomalies = observed_block - normal_block
    broad_layout = weights[None, :, None]
    skill_terms = jnp.stack(
        [
            jnp.sum(broad_layout * mismatch_parts * mismatch_parts, axis=(0, 1)),
            jnp.sum(broad_layout * predicted_anomalies * observed_anomalies, axis=(0, 1)),
            jnp.sum(broad_layout * predicted_anomalies * predicted_anomalies, axis=(0, 1)),
            jnp.sum(broad_layout * observed_anomalies * observed_anomalies, axis=(0, 1)),
        ]
    )
    predicted_meridians = predicted_block.transpose(0, 2, 1).reshape(
        meridian_lines, meridian_number
    )
    true_cols = observed_block.transpose(0, 2, 1).reshape(meridian_lines, meridian_number)
    full_table = dft_table(lon_total, lon_total, wave_count)
    fore_blocks = predicted_meridians.reshape(meridian_lines, lon_devices, row_share)
    true_blocks = true_cols.reshape(meridian_lines, lon_devices, row_share)
    fore_part = lax.all_to_all(fore_blocks, "lon", split_axis=1, concat_axis=0, tiled=True)[:, 0, :]
    true_part = lax.all_to_all(true_blocks, "lon", split_axis=1, concat_axis=0, tiled=True)[:, 0, :]
    items = fore_part.shape[1]
    stacked = jnp.concatenate([fore_part, true_part], axis=1)
    coeffs = transform_columns(stacked, full_table)
    powers = row_powers(coeffs[:items], coeffs[items:], wave_count)
    share_start = lax.axis_index("lon") * row_share
    global_cols = share_start + jnp.arange(row_share, dtype=jnp.int32)
    field_of = global_cols // parallel_lines
    row_weights = latitude_weights(lat_first + global_cols % parallel_lines, parallel_number)
    row_scale = row_weights / (lon_total * lon_total * weight_total)
    weighted = powers.reshape(row_share, 3 * wave_count) * row_scale[:, None]
    field_index = jnp.arange(quantity_labels, dtype=jnp.int32)
    window = min(quantity_labels, row_share // parallel_lines + 2)
    first_field = share_start // parallel_lines
    window_index = jnp.arange(window, dtype=jnp.int32)
    offset = field_of - first_field
    selector = (offset[None, :] == window_index[:, None]).astype(jnp.float32)
    band_sum = jnp.dot(
        selector, weighted, precision=lax.Precision.HIGHEST, preferred_element_type=jnp.float32
    )
    band_sum = lax.psum(band_sum, "lat")
    gathered = lax.all_gather(band_sum, "lon", axis=0, tiled=True)
    slot_index = jnp.arange(lon_devices * window, dtype=jnp.int32)
    slot_field = slot_index // window * row_share // parallel_lines + slot_index % window
    placer = (slot_field[None, :] == field_index[:, None]).astype(jnp.float32)
    summed = jnp.dot(
        placer, gathered, precision=lax.Precision.HIGHEST, preferred_element_type=jnp.float32
    )
    energy_curves = summed.reshape(quantity_labels, 3, wave_count).transpose(1, 0, 2)
    skill_means = lax.psum(skill_terms, ("lat", "lon")) / (lon_total * weight_total)
    rms_error = jnp.sqrt(skill_means[0])
    anomaly_corr = skill_means[1] / jnp.sqrt(
        (skill_means[2] + epsilon) * (skill_means[3] + epsilon)
    )
    return (energy_curves, rms_error, anomaly_corr)


def solution(mesh):
    in_specs = (P("lon", "lat"), P("lon", "lat"), P("lon", "lat"))
    out_specs = (P(), P(), P())
    return jax.shard_map(local, mesh=mesh, in_specs=in_specs, out_specs=out_specs, check_vma=False)
```

profile of v0, /device:TPU:8, one launch (start us, length us, event | category | flops | bytes accessed | tf_op | source)
XLA Modules:
  0.0 275.4 jit_solution(18060614692774121550)
XLA Ops:
  7.2 3.2 %copy.26 = f32[360,1664]{0,1:T(8,128)} copy(f32[360,1664]{1,0:T(8,128)} %param.4) | data formatting | bytes 4792320 | tf_op args[1]
  10.4 2.4 reshape.125
  12.8 1.9 copy.27
  14.8 0.0 copy-start
  14.8 4.8 %all-to-all-start.1 = ((f32[360,4,416]{0,2,1:T(8,128)}), f32[360,4,416]{0,2,1:T(8,128)}, u32[]{:S(2)}, u32[]{:S(2)}) async-start(f32[360,4,416]{0,2,1:T(8,128)} %bitcast.41), calls=%async_computation.1 | async-start | bytes 5111808 | tf_op jit(solution)/shard_map/all_to_all | solution.py:83
  19.5 0.0 copy-done
  19.6 2.2 copy.23
  21.7 2.4 reshape.124
  24.2 2.1 copy.24
  26.3 0.1 mul.170
  26.4 0.1 mul.171
  26.5 23.2 %all-to-all-done.1 = f32[360,4,416]{0,2,1:T(8,128)} async-done(((f32[360,4,416]{0,2,1:T(8,128)}), f32[360,4,416]{0,2,1:T(8,128)}, u32[]{:S(2)}, u32[]{:S(2)}) %all-to-all-start.1) | async-done | bytes 2396192 | tf_op jit(solution)/shard_map/all_to_all | solution.py:83
  49.7 3.6 %all-to-all-start = ((f32[360,4,416]{0,2,1:T(8,128)}), f32[360,4,416]{0,2,1:T(8,128)S(1)}, u32[]{:S(2)}, u32[]{:S(2)}) async-start(f32[360,4,416]{0,2,1:T(8,128)} %bitcast.39), calls=%async_computation | async-start | bytes 5111808 | tf_op jit(solution)/shard_map/all_to_all | solution.py:82
  53.3 0.0 all-reduce.2.cloned.1.call-start
  53.4 4.3 %fusion.17 = (f32[1664]{0:T(1024)S(1)}, f32[1664]{0:T(1024)S(1)}, f32[1664]{0:T(1024)S(1)}, f32[1664]{0:T(1024)S(1)}) fusion(f32[360,1664]{1,0:T(8,128)} %param.3, f32[360,1664]{1,0:T(8,128)} %param.4, f32[1664]{0:T(1024)S(1)} %mul.171, f32[360,1664]{1,0:T(8,128)} %param.5), kind=kLoop, calls=%fused_computation.26 | loop fusion | flops 8379904 | bytes 7221760 | tf_op jit(solution)/shard_map/reduce_sum | solution.py:69
  57.6 0.1 reduce_sum.84
  57.7 0.1 reduce_sum.81
  57.9 0.1 reduce_sum.62
  58.0 0.1 reduce_sum.59
  58.1 0.7 cosine_reduce_fusion
  60.1 55.8 %psum.15 = f32[4,52]{1,0:T(4,128)S(1)} all-reduce(f32[4,52]{1,0:T(4,128)S(1)} %pad_maximum_fusion.1), channel_id=1, replica_groups=mesh['lat'=8,'lon'=4] {'lat','lon'}, use_global_device_ids=true, to_apply=%region_10.11 | all-reduce | flops 208 | bytes 1664 | tf_op jit(solution)/shard_map/psum | solution.py:112
  115.9 0.1 fusion.37
  116.0 0.5 multiply_bitcast_fusion
  116.5 19.7 %sine_negate_fusion = (f32[1440,721]{1,0:T(8,128)}, f32[1440,721]{1,0:T(8,128)}) fusion(), kind=kLoop, calls=%fused_computation.12 | loop fusion | flops 10382400 | bytes 8305920 | tf_op jit(solution)/shard_map/neg | solution.py:19
  136.2 4.8 %copy.28 = f32[4,360,1,416]{1,0,3,2:T(4,128)} copy(f32[4,360,1,416]{1,3,0,2:T(8,128)} %bitcast.7) | data formatting | bytes 4792320 | tf_op jit(solution)/shard_map/all_to_all | solution.py:83
  141.1 4.0 %squeeze.5 = f32[1440,416]{0,1:T(8,128)} reshape(f32[4,360,1,416]{1,0,3,2:T(4,128)} %copy.28) | data formatting | bytes 4792320 | tf_op jit(solution)/shard_map/squeeze | solution.py:83
  145.1 0.0 all-to-all-done
  145.1 3.1 %copy.25 = f32[4,360,1,416]{1,0,3,2:T(4,128)} copy(f32[4,360,1,416]{1,3,0,2:T(8,128)S(1)} %bitcast.40) | data formatting | bytes 4792320 | tf_op jit(solution)/shard_map/all_to_all | solution.py:82
  148.2 0.0 copy-start.1
  148.2 4.2 %squeeze.4 = f32[1440,416]{0,1:T(8,128)} reshape(f32[4,360,1,416]{1,0,3,2:T(4,128)} %copy.25) | data formatting | bytes 4792320 | tf_op jit(solution)/shard_map/squeeze | solution.py:82
  152.4 0.0 copy-done.1
  152.4 29.4 %fusion = f32[832,1442]{1,0:T(8,128)S(1)} fusion(f32[1440,721]{1,0:T(8,128)} %get-tuple-element.20, f32[1440,721]{1,0:T(8,128)} %get-tuple-element.21, f32[1440,416]{0,1:T(8,128)S(1)} %copy-done.1, f32[1440,416]{0,1:T(8,128)} %squeeze.4), kind=kOutput, calls=%fused_computation | convolution fusion | flops 20734851072 | bytes 17897216 | tf_op jit(solution)/shard_map/dot_general | solution.py:23
  181.9 0.4 slice_subtract_fusion
  182.3 0.7 fusion.25
  183.0 0.4 fusion.21
  183.4 2.1 pad_maximum_fusion
  185.5 5.6 %copy.29 = f32[416,3,721]{0,2,1:T(8,128)} copy(f32[416,3,721]{2,0,1:T(8,128)} %pad_maximum_fusion) | data formatting | bytes 7198464 | tf_op jit(solution)/shard_map/stack | solution.py:41
  191.1 4.9 %reshape.126 = f32[416,2163]{0,1:T(8,128)} reshape(f32[416,3,721]{0,2,1:T(8,128)} %copy.29) | data formatting | bytes 7198464 | tf_op jit(solution)/shard_map/reshape | solution.py:93
  196.0 5.2 %fusion.7 = f32[15,2163]{1,0:T(8,128)} fusion(f32[416,2163]{0,1:T(8,128)} %reshape.126, f32[416]{0:T(512)S(1)} %fusion.37, s32[416]{0:T(512)S(1)} %fusion.29), kind=kOutput, calls=%fused_computation.8 | convolution fusion | flops 162871488 | bytes 3732340 | tf_op jit(solution)/shard_map/dot_general | solution.py:100
  201.2 0.0 all-reduce.2.cloned.1.call-update
  201.2 54.4 %all-reduce.2.cloned.1.call-done = f32[15,2163]{1,0:T(8,128)} async-done(((f32[15,2163]{1,0:T(8,128)}), f32[15,2163]{1,0:T(8,128)}) %all-reduce.2.cloned.1.call-update) | async-done | bytes 129796 | tf_op jit(solution)/shard_map/psum | solution.py:103
  255.6 11.1 %all-gather = f32[4,15,2163]{2,1,0:T(8,128)S(1)} all-gather(f32[1,15,2163]{2,1,0:T(8,128)} %bitcast.43), channel_id=1, replica_groups=mesh['lat'=8,'lon'=4] {'lon'}, dimensions={0}, use_global_device_ids=true | all-gather | bytes 648900 | tf_op jit(solution)/shard_map/all_gather | solution.py:104
  266.7 0.1 reshape.129
  266.8 0.4 fusion.26
  267.2 0.4 reshape.127
  267.7 0.9 copy.30
  (9 shorter events, 0.2 us)
Async XLA Ops:
  14.8 4.8 %copy-start = (f32[360,1664]{1,0:T(8,128)S(1)}, f32[360,1664]{1,0:T(8,128)}, u32[]{:S(2)}) copy-start(f32[360,1664]{1,0:T(8,128)} %param.3) | copy-start | bytes 7188484
  14.8 34.9 %all-to-all-start.1 = ((f32[360,4,416]{0,2,1:T(8,128)}), f32[360,4,416]{0,2,1:T(8,128)}, u32[]{:S(2)}, u32[]{:S(2)}) async-start(f32[360,4,416]{0,2,1:T(8,128)} %bitcast.41), calls=%async_computation.1 | async-start | bytes 5111808 | tf_op jit(solution)/shard_map/all_to_all | solution.py:83
  49.7 95.4 %all-to-all-start = ((f32[360,4,416]{0,2,1:T(8,128)}), f32[360,4,416]{0,2,1:T(8,128)S(1)}, u32[]{:S(2)}, u32[]{:S(2)}) async-start(f32[360,4,416]{0,2,1:T(8,128)} %bitcast.39), calls=%async_computation | async-start | bytes 5111808 | tf_op jit(solution)/shard_map/all_to_all | solution.py:82
  53.3 202.3 %all-reduce.2.cloned.1.call-start = ((), (), s32[]{:S(2)}) async-start(), calls=%async_computation.2 | async-start | bytes 278528 | tf_op jit(solution)/shard_map/psum | solution.py:103
  148.2 4.2 %copy-start.1 = (f32[1440,416]{0,1:T(8,128)S(1)}, f32[1440,416]{0,1:T(8,128)}, u32[]{:S(2)}) copy-start(f32[1440,416]{0,1:T(8,128)} %squeeze.5) | copy-start | bytes 7188484
Sparse Core Ops, SparseCore 0:
  201.3 54.3 all-reduce.1
where the time goes:
time: 276 us; the launch traced here: 275 us
  waiting for transfers between devices  77.7 us (28%)
  blocking collectives  66.9 us (24%)
  local copies, waits for them, and re-layouts  42.9 us (16%)
  matrix products  35 us (13%)
  other arithmetic  29 us (11%)
  between operations  15.5 us (6%)
  starting transfers between devices  8.44 us (3%)
    psum x1, blocking collectives, local(): lax.psum(skill_terms, ('lat', 'lon')) / (lon_total * weight_total)  55.8 us
    psum x1, waiting for transfers between devices, local(): band_sum = lax.psum(band_sum, 'lat')  54.4 us
    dot_general x1, matrix products, transform_columns(): lax.dot_general(stacked, table, (((0,), (0,)), ((), ())), precision=lax.P...  29.4 us
    all_to_all x1, waiting for transfers between devices, local(): lax.all_to_all(true_blocks, 'lon', split_axis=1, concat_axis=0, tiled=True)  23.2 us
    neg x1, other arithmetic, dft_table(): return jnp.concatenate([jnp.cos(angle), -jnp.sin(angle)], axis=1)  19.7 us
    all_gather x1, blocking collectives, local(): gathered = lax.all_gather(band_sum, 'lon', axis=0, tiled=True)  11.1 us
    unnamed x8, local copies, waits for them, and re-layouts  6.34 us
    another operation x1, local copies, waits for them, and re-layouts, row_powers(): jnp.stack([square(fore_coeffs), square(true_coeffs), square(diff_coeffs)]...  5.61 us
  transfers between devices with their start and end apart: 3, of which 2 were waited for; matrix products, arithmetic and copies ran while one was open for 15% of the time, Pallas kernels for 0%

commit v1 on v0

--- a/solution.py
+++ b/solution.py
@@ -100,7 +100,11 @@
     band_sum = jnp.dot(
         selector, weighted, precision=lax.Precision.HIGHEST, preferred_element_type=jnp.float32
     )
-    band_sum = lax.psum(band_sum, "lat")
+    size, total = (lax.axis_size("lat"), band_sum)
+    for far in [1 << k for k in range(size.bit_length() - 1)]:
+        swap = [(i, i ^ far) for i in range(size)]
+        total = total + lax.ppermute(total, "lat", swap)
+    band_sum = total
     gathered = lax.all_gather(band_sum, "lon", axis=0, tiled=True)
     slot_index = jnp.arange(lon_devices * window, dtype=jnp.int32)
     slot_field = slot_index // window * row_share // parallel_lines + slot_index % window

time: 276 us -> 205 us (0.74)
  waiting for transfers between devices: 77.7 us -> 32.2 us
  blocking collectives: 66.9 us -> 51.8 us
  between operations: 15.5 us -> 2.14 us
    psum x1 -> x0, waiting for transfers between devices: 54.4 us -> none  [local(): band_sum = lax.psum(band_sum, 'lat')]
    psum x1, blocking collectives: 55.8 us -> 40.9 us  [local(): lax.psum(skill_terms, ('lat', 'lon')) / (lon_total * weight_total)]
    ppermute x0 -> x3, waiting for transfers between devices: none -> 8.8 us  [local(): total = total + lax.ppermute(total, 'lat', swap)]
    unnamed x8 -> x12, local copies, waits for them, and re-layouts: 6.34 us -> 6.35 us
  transfers between devices with their start and end apart: 3 -> 5, of which waited for: 2 -> 3; matrix products, arithmetic and copies ran while one was open for 15% -> 20% of each run, Pallas kernels for 0% -> 0%
where the time goes in v1:
time: 205 us; the launch traced here: 202 us
  blocking collectives  51.8 us (25%)
  local copies, waits for them, and re-layouts  43 us (21%)
  matrix products  34.5 us (17%)
  waiting for transfers between devices  32.2 us (16%)
  other arithmetic  27.6 us (13%)
  starting transfers between devices  10.3 us (5%)
  between operations  2.14 us (1%)
    psum x1, blocking collectives, local(): lax.psum(skill_terms, ('lat', 'lon')) / (lon_total * weight_total)  40.9 us
    dot_general x1, matrix products, transform_columns(): lax.dot_general(stacked, table, (((0,), (0,)), ((), ())), precision=lax.P...  29.4 us
    all_to_all x1, waiting for transfers between devices, local(): lax.all_to_all(true_blocks, 'lon', split_axis=1, concat_axis=0, tiled=True)  23.4 us
    neg x1, other arithmetic, dft_table(): return jnp.concatenate([jnp.cos(angle), -jnp.sin(angle)], axis=1)  19.7 us
    all_gather x1, blocking collectives, local(): gathered = lax.all_gather(band_sum, 'lon', axis=0, tiled=True)  10.9 us
    ppermute x3, waiting for transfers between devices, local(): total = total + lax.ppermute(total, 'lat', swap)  8.8 us
    unnamed x12, local copies, waits for them, and re-layouts  6.35 us
    another operation x1, local copies, waits for them, and re-layouts, row_powers(): jnp.stack([square(fore_coeffs), square(true_coeffs), square(diff_coeffs)]...  5.61 us
  transfers between devices with their start and end apart: 5, of which 3 were waited for; matrix products, arithmetic and copies ran while one was open for 20% of the time, Pallas kernels for 0%

profile of v1, /device:TPU:8, one launch (start us, length us, event | category | flops | bytes accessed | tf_op | source)
XLA Modules:
  0.0 201.7 jit_solution(15554190356681933000)
XLA Ops:
  0.6 3.2 %copy.26 = f32[360,1664]{0,1:T(8,128)} copy(f32[360,1664]{1,0:T(8,128)} %param.4) | data formatting | bytes 4792320 | tf_op args[1]
  3.9 2.4 %reshape.125 = f32[360,32,52]{0,2,1:T(8,128)S(1)} reshape(f32[360,1664]{0,1:T(8,128)} %copy.26) | data formatting | bytes 4792320 | tf_op jit(solution)/shard_map/reshape | solution.py:61
  6.3 1.9 copy.27
  8.2 4.8 %all-to-all-start.1 = ((f32[360,4,416]{0,2,1:T(8,128)}), f32[360,4,416]{0,2,1:T(8,128)}, u32[]{:S(2)}, u32[]{:S(2)}) async-start(f32[360,4,416]{0,2,1:T(8,128)} %bitcast.42), calls=%async_computation.1 | async-start | bytes 5111808 | tf_op jit(solution)/shard_map/all_to_all | solution.py:83
  13.0 0.0 copy-done.1
  13.0 2.2 %copy.23 = f32[360,1664]{0,1:T(8,128)} copy(f32[360,1664]{1,0:T(8,128)S(1)} %copy-done.1) | data formatting | bytes 4792320 | tf_op args[0]
  15.2 2.4 %reshape.124 = f32[360,32,52]{0,2,1:T(8,128)S(1)} reshape(f32[360,1664]{0,1:T(8,128)} %copy.23) | data formatting | bytes 4792320 | tf_op jit(solution)/shard_map/reshape | solution.py:60
  17.6 2.1 %copy.24 = f32[360,52,32]{0,2,1:T(8,128)} copy(f32[360,52,32]{0,1,2:T(8,128)S(1)} %bitcast.39) | data formatting | bytes 4792320 | tf_op jit(solution)/shard_map/transpose | solution.py:75
  19.7 23.4 %all-to-all-done.1 = f32[360,4,416]{0,2,1:T(8,128)} async-done(((f32[360,4,416]{0,2,1:T(8,128)}), f32[360,4,416]{0,2,1:T(8,128)}, u32[]{:S(2)}, u32[]{:S(2)}) %all-to-all-start.1) | async-done | bytes 2396192 | tf_op jit(solution)/shard_map/all_to_all | solution.py:83
  43.1 3.6 %all-to-all-start = ((f32[360,4,416]{0,2,1:T(8,128)}), f32[360,4,416]{0,2,1:T(8,128)S(1)}, u32[]{:S(2)}, u32[]{:S(2)}) async-start(f32[360,4,416]{0,2,1:T(8,128)} %bitcast.40), calls=%async_computation | async-start | bytes 5111808 | tf_op jit(solution)/shard_map/all_to_all | solution.py:82
  46.8 0.1 mul.170
  46.9 0.1 mul.171
  47.0 0.6 cosine_reduce_fusion
  48.3 0.1 fusion.37
  48.4 19.7 %sine_negate_fusion = (f32[1440,721]{1,0:T(8,128)}, f32[1440,721]{1,0:T(8,128)}) fusion(), kind=kLoop, calls=%fused_computation.12 | loop fusion | flops 10382400 | bytes 8305920 | tf_op jit(solution)/shard_map/neg | solution.py:19
  68.1 4.8 %copy.28 = f32[4,360,1,416]{1,0,3,2:T(4,128)} copy(f32[4,360,1,416]{1,3,0,2:T(8,128)} %bitcast.7) | data formatting | bytes 4792320 | tf_op jit(solution)/shard_map/all_to_all | solution.py:83
  72.9 4.0 %squeeze.5 = f32[1440,416]{0,1:T(8,128)} reshape(f32[4,360,1,416]{1,0,3,2:T(4,128)} %copy.28) | data formatting | bytes 4792320 | tf_op jit(solution)/shard_map/squeeze | solution.py:83
  77.0 0.0 all-to-all-done
  77.0 3.1 %copy.25 = f32[4,360,1,416]{1,0,3,2:T(4,128)} copy(f32[4,360,1,416]{1,3,0,2:T(8,128)S(1)} %bitcast.41) | data formatting | bytes 4792320 | tf_op jit(solution)/shard_map/all_to_all | solution.py:82
  80.1 4.2 %squeeze.4 = f32[1440,416]{0,1:T(8,128)} reshape(f32[4,360,1,416]{1,0,3,2:T(4,128)} %copy.25) | data formatting | bytes 4792320 | tf_op jit(solution)/shard_map/squeeze | solution.py:82
  84.3 0.0 copy-done.3
  84.3 29.4 %fusion = f32[832,1442]{1,0:T(8,128)S(1)} fusion(f32[1440,721]{1,0:T(8,128)} %get-tuple-element.20, f32[1440,721]{1,0:T(8,128)} %get-tuple-element.21, f32[1440,416]{0,1:T(8,128)S(1)} %copy-done.3, f32[1440,416]{0,1:T(8,128)} %squeeze.4), kind=kOutput, calls=%fused_computation | convolution fusion | flops 20734851072 | bytes 17897216 | tf_op jit(solution)/shard_map/dot_general | solution.py:23
  113.7 0.4 slice_subtract_fusion
  114.2 0.7 fusion.25
  114.9 0.4 fusion.21
  115.3 2.1 %pad_maximum_fusion = f32[416,3,721]{2,0,1:T(8,128)} fusion(f32[416,1,721]{2,0,1:T(8,128)S(1)} %fusion.21, f32[416,1,721]{2,0,1:T(8,128)S(1)} %get-tuple-element.17, f32[416,1,721]{2,0,1:T(8,128)S(1)} %get-tuple-element.16), kind=kLoop, calls=%fused_computation.18 | loop fusion | flops 1799616 | bytes 7198464 | tf_op jit(solution)/shard_map/stack | solution.py:41
  117.4 5.6 %copy.29 = f32[416,3,721]{0,2,1:T(8,128)} copy(f32[416,3,721]{2,0,1:T(8,128)} %pad_maximum_fusion) | data formatting | bytes 7198464 | tf_op jit(solution)/shard_map/stack | solution.py:41
  123.0 5.0 %reshape.126 = f32[416,2163]{0,1:T(8,128)} reshape(f32[416,3,721]{0,2,1:T(8,128)} %copy.29) | data formatting | bytes 7198464 | tf_op jit(solution)/shard_map/reshape | solution.py:93
  128.0 4.6 %fusion.7 = f32[15,2163]{1,0:T(8,128)S(1)} fusion(f32[416,2163]{0,1:T(8,128)} %reshape.126, f32[416]{0:T(512)S(1)} %fusion.37, s32[416]{0:T(512)S(1)} %fusion.29), kind=kOutput, calls=%fused_computation.8 | convolution fusion | flops 162871488 | bytes 3732340 | tf_op jit(solution)/shard_map/dot_general | solution.py:100
  132.7 0.0 collective-permute-start
  132.7 0.0 copy-done.2
  132.7 2.8 %fusion.17 = (f32[1664]{0:T(1024)S(1)}, f32[1664]{0:T(1024)S(1)}, f32[1664]{0:T(1024)S(1)}, f32[1664]{0:T(1024)S(1)}) fusion(f32[360,1664]{1,0:T(8,128)S(1)} %copy-done.2, f32[360,1664]{1,0:T(8,128)S(1)} %copy-done, f32[1664]{0:T(1024)S(1)} %mul.171, f32[360,1664]{1,0:T(8,128)} %param.5), kind=kLoop, calls=%fused_computation.26 | loop fusion | flops 8379904 | bytes 7221760 | tf_op jit(solution)/shard_map/reduce_sum | solution.py:69
  135.5 0.1 reduce_sum.84
  135.6 0.1 reduce_sum.81
  135.8 0.1 reduce_sum.62
  135.9 0.1 reduce_sum.59
  136.7 40.9 %psum.7 = f32[4,52]{1,0:T(4,128)S(1)} all-reduce(f32[4,52]{1,0:T(4,128)S(1)} %pad_maximum_fusion.1), channel_id=1, replica_groups=mesh['lat'=8,'lon'=4] {'lat','lon'}, use_global_device_ids=true, to_apply=%region_9.10 | all-reduce | flops 208 | bytes 1664 | tf_op jit(solution)/shard_map/psum | solution.py:116
  177.6 0.0 collective-permute-done
  177.6 0.6 collective-permute-start.1
  178.2 4.5 %collective-permute-done.1 = f32[15,2163]{1,0:T(8,128)S(1)} collective-permute-done((f32[15,2163]{1,0:T(8,128)S(1)}, f32[15,2163]{1,0:T(8,128)S(1)}, u32[]{:S(2)}, u32[]{:S(2)}) %collective-permute-start.1) | collective-permute-done | bytes 129812 | tf_op jit(solution)/shard_map/ppermute | solution.py:106
  182.8 1.3 collective-permute-start.2
  184.1 0.5 multiply_bitcast_fusion
  184.6 4.3 %collective-permute-done.2 = f32[15,2163]{1,0:T(8,128)S(1)} collective-permute-done((f32[15,2163]{1,0:T(8,128)S(1)}, f32[15,2163]{1,0:T(8,128)S(1)}, u32[]{:S(2)}, u32[]{:S(2)}) %collective-permute-start.2) | collective-permute-done | bytes 129812 | tf_op jit(solution)/shard_map/ppermute | solution.py:106
  188.9 10.9 %all-gather = f32[4,15,2163]{2,1,0:T(8,128)S(1)} all-gather(f32[1,15,2163]{2,1,0:T(8,128)S(1)} %add_bitcast_fusion), channel_id=1, replica_groups=mesh['lat'=8,'lon'=4] {'lon'}, dimensions={0}, use_global_device_ids=true | all-gather | bytes 648900 | tf_op jit(solution)/shard_map/all_gather | solution.py:108
  199.9 0.1 reshape.129
  199.9 0.4 fusion.26
  200.4 0.4 reshape.127
  200.8 0.9 copy.30
  (17 shorter events, 0.2 us)
Async XLA Ops:
  8.2 4.8 %copy-start.1 = (f32[360,1664]{1,0:T(8,128)S(1)}, f32[360,1664]{1,0:T(8,128)}, u32[]{:S(2)}) copy-start(f32[360,1664]{1,0:T(8,128)} %param.3) | copy-start | bytes 7188484
  8.2 34.9 %all-to-all-start.1 = ((f32[360,4,416]{0,2,1:T(8,128)}), f32[360,4,416]{0,2,1:T(8,128)}, u32[]{:S(2)}, u32[]{:S(2)}) async-start(f32[360,4,416]{0,2,1:T(8,128)} %bitcast.42), calls=%async_computation.1 | async-start | bytes 5111808 | tf_op jit(solution)/shard_map/all_to_all | solution.py:83
  43.1 33.9 %all-to-all-start = ((f32[360,4,416]{0,2,1:T(8,128)}), f32[360,4,416]{0,2,1:T(8,128)S(1)}, u32[]{:S(2)}, u32[]{:S(2)}) async-start(f32[360,4,416]{0,2,1:T(8,128)} %bitcast.40), calls=%async_computation | async-start | bytes 5111808 | tf_op jit(solution)/shard_map/all_to_all | solution.py:82
  80.1 4.2 %copy-start.3 = (f32[1440,416]{0,1:T(8,128)S(1)}, f32[1440,416]{0,1:T(8,128)}, u32[]{:S(2)}) copy-start(f32[1440,416]{0,1:T(8,128)} %squeeze.5) | copy-start | bytes 7188484
  123.0 9.7 %copy-start.2 = (f32[360,1664]{1,0:T(8,128)S(1)}, f32[360,1664]{1,0:T(8,128)}, u32[]{:S(2)}) copy-start(f32[360,1664]{1,0:T(8,128)} %param.3) | copy-start | bytes 7188484
  128.0 4.7 %copy-start = (f32[360,1664]{1,0:T(8,128)S(1)}, f32[360,1664]{1,0:T(8,128)}, u32[]{:S(2)}) copy-start(f32[360,1664]{1,0:T(8,128)} %param.4) | copy-start | bytes 7188484
  132.7 44.9 %collective-permute-start = (f32[15,2163]{1,0:T(8,128)S(1)}, f32[15,2163]{1,0:T(8,128)S(1)}, u32[]{:S(2)}, u32[]{:S(2)}) collective-permute-start(f32[15,2163]{1,0:T(8,128)S(1)} %fusion.7), channel_id=1, source_target_pairs={{0,4},{4,0},{8,12},{12,8},{16,20},{20,16},{24,28},{28,24},{1,5},{5... | collective-permute-start | bytes 389348 | tf_op jit(solution)/shard_map/ppermute | solution.py:106
  177.6 5.1 %collective-permute-start.1 = (f32[15,2163]{1,0:T(8,128)S(1)}, f32[15,2163]{1,0:T(8,128)S(1)}, u32[]{:S(2)}, u32[]{:S(2)}) collective-permute-start(f32[15,2163]{1,0:T(8,128)S(1)} %add.154), channel_id=1, source_target_pairs={{0,8},{4,12},{8,0},{12,4},{16,24},{20,28},{24,16},{28,20},{1,9},{5... | collective-permute-start | bytes 389348 | tf_op jit(solution)/shard_map/ppermute | solution.py:106
  182.8 6.1 %collective-permute-start.2 = (f32[15,2163]{1,0:T(8,128)S(1)}, f32[15,2163]{1,0:T(8,128)S(1)}, u32[]{:S(2)}, u32[]{:S(2)}) collective-permute-start(f32[15,2163]{1,0:T(8,128)S(1)} %add.155), channel_id=1, source_target_pairs={{0,16},{4,20},{8,24},{12,28},{16,0},{20,4},{24,8},{28,12},{1,17},{... | collective-permute-start | bytes 389348 | tf_op jit(solution)/shard_map/ppermute | solution.py:106
